TPU v7x, 32 devices: a whole 2x2x4 slice. The times are simulated.
32 devices in a mesh: row: 4 (over z), col: 8 (over y, x, core).
Axes of the slice: x: 2, y: 2, z: 4, core: 2. Of those that a mesh axis runs over, the one named last changes fastest.
Arguments:
- features: bfloat16 [12288, 128], P(('row', 'col')), may hold values from -6 to 6
- weight: bfloat16 [128, 128], replicated, may hold values from -0.5 to 0.5
- tiles: bfloat16 [4, 2048, 128, 128], P('row', 'col'), may hold values from -0.09375 to 0.09375
- tile_dest: int32 [4, 2048], P('row', 'col'), may hold values from 0 to 23, as said below
- tile_src: int32 [4, 2048], P('row', 'col'), may hold values from 0 to 11, as said below
- tile_count: int32 [4, 8], P('row', 'col'), may hold values from 32 to 256, as said below
- source_of: int32 [12288], P(('row', 'col')), may hold values from 0 to 12287, as said below
- out_grad: bfloat16 [12288, 128], P(('row', 'col')), may hold values from -6 to 6
Outputs:
- activations: bfloat16 [12288, 128], P(('row', 'col'))
- feature_grad: bfloat16 [12288, 128], P(('row', 'col'))
- weight_grad: float32 [128, 128], replicated
Inputs may be any that keep to these rules, and one draw needn't show every extreme that they name: `tile_dest`: the slots of one device name distinct tiles. `tile_src`: the slots of one device name distinct tiles. `tile_count`: some device has all of its 256 slots live. `source_of`: a permutation of the 12288 vertices; of the 384 destination positions of each device, exactly 12 hold source vertices of each device.
All inputs are finite; a program needn't handle non-finite values.
Results may differ from a plain program's by a relative error of at most 0.017.
Values may be sent and summed in bfloat16 or wider, within the bound.
No kernel may reach another device: no remote copies, remote signals or barrier semaphores. Data moves between devices by JAX's collectives and lax.ppermute only.
A program may use at most 64 MiB of HBM per device.

v0:
```python
import math
import jax
import jax.numpy as jnp
from jax import lax
from jax.sharding import PartitionSpec as P


def silu_slope(values):
    sigma = jax.nn.sigmoid(values)
    return sigma * (1.0 + values * (1.0 - sigma))


def tile_products(tile_set, dest_index, source_index, live_count, operand, out_blocks, transposed):
    tile_edge = tile_set.shape[-1]
    feat_width = operand.shape[-1]
    block_size = math.gcd(tile_set.shape[0], 32)
    operand_blocks = operand.reshape(-1, tile_edge, feat_width)
    step_count = (live_count + block_size - 1) // block_size

    def add_block(block_step, totals):
        first_slot = block_step * block_size
        tile_block = lax.dynamic_slice_in_dim(tile_set, first_slot, block_size, 0)
        dest_block = lax.dynamic_slice_in_dim(dest_index, first_slot, block_size, 0)
        source_block = lax.dynamic_slice_in_dim(source_index, first_slot, block_size, 0)
        live_mask = first_slot + jnp.arange(block_size) < live_count
        if transposed:
            product = jnp.einsum(
                "bji,bjf->bif",
                tile_block,
                operand_blocks[dest_block],
                preferred_element_type=jnp.float32,
            )
            target = source_block
        else:
            product = jnp.einsum(
                "bij,bjf->bif",
                tile_block,
                operand_blocks[source_block],
                preferred_element_type=jnp.float32,
            )
            target = dest_block
        product = jnp.where(live_mask[:, None, None], product, 0.0)
        return totals.at[target].add(product)

    totals = jnp.zeros((out_blocks, tile_edge, feat_width), jnp.float32)
    totals = lax.fori_loop(0, step_count, add_block, totals)
    return totals.reshape(-1, feat_width)


def local(features, weight, tiles, tile_dest, tile_src, tile_count, source_of, out_grad):
    shard_rows, feat_width = features.shape
    tile_edge = tiles.shape[-1]
    group_total = lax.axis_size(("row", "col"))
    strip_total = lax.axis_size("row")
    column_total = lax.axis_size("col")
    live_count = tile_count[0, 0]
    hidden = jnp.dot(features, weight, preferred_element_type=jnp.float32).astype(jnp.bfloat16)
    group_rows = lax.all_gather(hidden, "row", axis=0, tiled=True)
    partial_value = tile_products(
        tiles[0],
        tile_dest[0],
        tile_src[0],
        live_count,
        group_rows,
        column_total * shard_rows // tile_edge,
        False,
    )
    own_base = lax.axis_index(("row", "col")) * shard_rows
    summed = lax.psum_scatter(
        partial_value.astype(jnp.bfloat16), "col", scatter_dimension=0, tiled=True
    )
    row_owner = source_of // shard_rows
    send_order = jnp.argsort(row_owner, stable=True)
    got_rows, got_ids = (
        lax.all_to_all(summed[send_order], ("row", "col"), split_axis=0, concat_axis=0, tiled=True),
        lax.all_to_all(
            source_of[send_order], ("row", "col"), split_axis=0, concat_axis=0, tiled=True
        ),
    )
    local_ids = got_ids - own_base
    act_rows = jax.nn.silu(got_rows.astype(jnp.float32)).astype(jnp.bfloat16)
    activations = jnp.zeros((shard_rows, feat_width), jnp.bfloat16).at[local_ids].set(act_rows)
    returned = lax.all_to_all(
        out_grad[local_ids], ("row", "col"), split_axis=0, concat_axis=0, tiled=True
    )
    dest_grad = jnp.zeros((shard_rows, feat_width), jnp.bfloat16).at[send_order].set(returned)
    pre_float = summed.astype(jnp.float32)
    local_grad = (dest_grad.astype(jnp.float32) * silu_slope(pre_float)).astype(jnp.bfloat16)
    strip_grad = lax.all_gather(local_grad, "col", axis=0, tiled=True)
    group_partial = tile_products(
        tiles[0],
        tile_dest[0],
        tile_src[0],
        live_count,
        strip_grad,
        strip_total * shard_rows // tile_edge,
        True,
    )
    source_part = lax.psum_scatter(
        group_partial.astype(jnp.bfloat16), "row", scatter_dimension=0, tiled=True
    )
    feature_grad = jnp.dot(source_part, weight.T, preferred_element_type=jnp.float32).astype(
        jnp.bfloat16
    )
    weight_part = jnp.dot(features.T, source_part, preferred_element_type=jnp.float32)
    weight_grad = lax.psum(weight_part, ("row", "col")) * (
        1.0 / math.sqrt(shard_rows * group_total)
    )
    return (activations, feature_grad, weight_grad)


def solution(mesh):
    placed = (
        P(("row", "col"), None),
        P(),
        P("row", "col", None, None),
        P("row", "col"),
        P("row", "col"),
        P("row", "col"),
        P(("row", "col")),
        P(("row", "col"), None),
    )
    return jax.shard_map(
        local,
        mesh=mesh,
        in_specs=placed,
        out_specs=(P(("row", "col"), None), P(("row", "col"), None), P()),
        check_vma=False,
    )
```

profile of v0, /device:TPU:1, one launch (start us, length us, event | category | flops | bytes accessed | tf_op | source)
XLA Modules:
  0.0 383.0 jit_solution(3259870633152334014)
XLA Ops:
  8.1 0.9 convolution_convert_fusion.1
  9.0 14.6 %all_gather.6 = bf16[1536,128]{1,0:T(8,128)(2,1)} all-gather(bf16[384,128]{1,0:T(8,128)(2,1)S(1)} %convolution_convert_fusion.1), channel_id=1, replica_groups=mesh['row'=4,'col'=8] {'row'}, dimensions={0}, use_global_device_ids=true | all-gather | bytes 491520 | tf_op jit(solution)/shard_map/all_gather | solution.py:58
  23.6 1.3 broadcast_in_dim.48
  25.0 10.2 %while.20 = (s32[]{:T(128)}, f32[24,128,128]{2,1,0:T(8,128)}, s32[]{:T(128)}, s32[256]{0:T(256)S(1)}, s32[]{:T(128)}, /*index=5*/bf16[256,128,128]{2,1,0:T(8,128...) while((s32[]{:T(128)}, f32[24,128,128]{2,1,0:T(8,128)}, ...), condition=%wide.region_3.4_spmd, body=%wide.region_1.3_spmd.sunk | while | flops 135267584 | bytes 12588147 | solution.py:46
  25.7 1.7 gather_fusion
  27.5 1.7 convolution_select_fusion.4
  29.1 6.1 %scatter_fusion = f32[24,128,128]{2,1,0:T(8,128)} fusion(f32[24,128,128]{2,1,0:T(8,128)} %get-tuple-element.283, s32[32]{0:T(128)S(1)} %get-tuple-element.258, f32[32,128,128]{2,1,0:T(8,128)S(1)} %convolution_select_fusion.4), kind=kCustom, calls=%fused_computation.5.clone.1 | custom fusion | flops 524288 | bytes 6291584 | tf_op jit(solution)/shard_map/while/body/scatter-add | solution.py:43
  35.2 2.5 convert_element_type.37
  37.8 3.8 sort.17
  41.5 2.8 gather_fusion.2
  45.1 78.3 %all-to-all-start = ((s32[32,12,1]{1,2,0:T(1,128)}), s32[32,12,1]{1,2,0:T(1,128)S(1)}, u32[]{:S(2)}, u32[]{:S(2)}) async-start(s32[32,12,1]{1,2,0:T(1,128)} %bitcast), calls=%async_computation | async-start | bytes 32768 | tf_op jit(solution)/shard_map/all_to_all | solution.py:76
  123.4 6.7 %all-to-all-done = s32[32,12,1]{1,2,0:T(1,128)S(1)} async-done(((s32[32,12,1]{1,2,0:T(1,128)}), s32[32,12,1]{1,2,0:T(1,128)S(1)}, u32[]{:S(2)}, u32[]{:S(2)}) %all-to-all-start) | async-done | bytes 1568 | tf_op jit(solution)/shard_map/all_to_all | solution.py:76
  130.3 1.4 gather_fusion.4
  132.5 2.8 all-to-all-start.2
  135.3 12.0 %copy.18 = bf16[1,256,128,128]{2,3,1,0:T(8,128)(2,1)} copy(bf16[1,256,128,128]{3,2,1,0:T(8,128)(2,1)} %bitcast.28) | data formatting | bytes 16777216 | tf_op args[2]
  147.3 1.5 scatter_custom_fusion.3
  148.8 1.0 fusion.10
  149.8 11.8 %all_gather.7 = bf16[3072,128]{1,0:T(8,128)(2,1)} all-gather(bf16[384,128]{1,0:T(8,128)(2,1)S(1)} %fusion.10), channel_id=1, replica_groups=mesh['row'=4,'col'=8] {'col'}, dimensions={0}, use_global_device_ids=true | all-gather | bytes 884736 | tf_op jit(solution)/shard_map/all_gather | solution.py:89
  161.7 8.3 %while.21 = (s32[]{:T(128)}, f32[12,128,128]{2,1,0:T(8,128)S(1)}, s32[]{:T(128)}, s32[256]{0:T(256)S(1)}, s32[]{:T(128)}, /*index=5*/bf16[256,128,128]{1,2,0:T(8...) while((s32[]{:T(128)}, f32[12,128,128]{2,1,0:T(8,128)S(1)}, ...), condition=%wide.region_9.10_spmd, body=%wide.region_7.9_spmd.sunk | while | flops 135267584 | bytes 12588147 | solution.py:46
  162.5 2.9 gather_fusion.1
  165.4 2.0 convolution_select_fusion.5
  167.4 2.7 scatter_fusion.1
  170.1 0.8 convert_element_type.45
  171.0 1.4 gather_fusion.3
  172.4 71.0 %all_to_all.30 = bf16[32,12,128]{2,1,0:T(8,128)(2,1)S(1)} all-to-all(bf16[32,12,128]{2,1,0:T(8,128)(2,1)S(1)} %all_to_all.22), channel_id=1, replica_groups=mesh['row'=4,'col'=8] {'row','col'}, dimensions={0} | all-to-all | bytes 196608 | tf_op jit(solution)/shard_map/all_to_all | solution.py:75
  243.5 2.1 scatter_custom_fusion.2
  245.6 0.9 reduce-scatter.5.cloned.1.call-done
  246.5 1.7 convolution_bitcast_fusion
  248.2 1.7 convolution_convert_fusion
  249.9 124.9 %all-reduce.2.cloned.1.call-done = f32[128,128]{0,1:T(8,128)} async-done(((f32[128,128]{0,1:T(8,128)}), f32[128,128]{0,1:T(8,128)}) %all-reduce.2.cloned.1.call-update) | async-done | bytes 65552 | tf_op jit(solution)/shard_map/psum | solution.py:106
  374.8 0.8 broadcast_multiply_fusion
  375.7 0.7 copy.20
  (42 shorter events, 3.6 us)
Async XLA Ops:
  7.2 0.9 copy-start
  7.2 17.8 %copy-start.6 = (s32[1,256]{1,0:T(1,128)S(1)}, s32[1,256]{1,0:T(1,128)}, u32[]{:S(2)}) copy-start(s32[1,256]{1,0:T(1,128)} %param.16) | copy-start | bytes 3076
  7.2 17.8 %copy-start.5 = (s32[1,256]{1,0:T(1,128)S(1)}, s32[1,256]{1,0:T(1,128)}, u32[]{:S(2)}) copy-start(s32[1,256]{1,0:T(1,128)} %param.15) | copy-start | bytes 3076
  7.2 141.6 %reduce-scatter.3.cloned.1.call-start = ((), (), s32[]{:S(2)}) async-start(), calls=%async_computation.5 | async-start | bytes 884736 | tf_op jit(solution)/shard_map/reduce_scatter | solution.py:69
  35.2 2.5 copy-start.1
  37.7 92.6 %copy-start.3 = (bf16[384,128]{1,0:T(8,128)(2,1)S(1)}, bf16[384,128]{1,0:T(8,128)(2,1)}, u32[]{:S(2)}) copy-start(bf16[384,128]{1,0:T(8,128)(2,1)} %param.19) | copy-start | bytes 294916
  45.1 85.1 %all-to-all-start = ((s32[32,12,1]{1,2,0:T(1,128)}), s32[32,12,1]{1,2,0:T(1,128)S(1)}, u32[]{:S(2)}, u32[]{:S(2)}) async-start(s32[32,12,1]{1,2,0:T(1,128)} %bitcast), calls=%async_computation | async-start | bytes 32768 | tf_op jit(solution)/shard_map/all_to_all | solution.py:76
  132.5 14.8 %all-to-all-start.2 = ((bf16[32,12,128]{2,1,0:T(8,128)(2,1)}), bf16[32,12,128]{2,1,0:T(8,128)(2,1)S(1)}, u32[]{:S(2)}, u32[]{:S(2)}) async-start(bf16[32,12,128]{2,1,0:T(8,128)(2,1)} %all_to_all.24), calls=%async_computation.3 | async-start | bytes 262144 | tf_op jit(solution)/shard_map/all_to_all | solution.py:83
  135.3 111.2 %reduce-scatter.5.cloned.1.call-start = ((), (), s32[]{:S(2)}) async-start(), calls=%async_computation.6 | async-start | bytes 491520 | tf_op jit(solution)/shard_map/reduce_scatter | solution.py:99
  170.0 0.9 copy-start.2
  170.0 78.2 %copy-start.4 = (bf16[128,128]{1,0:T(8,128)(2,1)S(1)}, bf16[128,128]{1,0:T(8,128)(2,1)}, u32[]{:S(2)}) copy-start(bf16[128,128]{1,0:T(8,128)(2,1)} %param.13) | copy-start | bytes 98308
  170.9 204.0 %all-reduce.2.cloned.1.call-start = ((), (), s32[]{:S(2)}) async-start(), calls=%async_computation.7 | async-start | bytes 131072 | tf_op jit(solution)/shard_map/psum | solution.py:106
Sparse Core Ops, SparseCore 0:
  37.8 107.7 reduce-scatter.2
  171.0 75.4 reduce-scatter.4
  252.6 122.1 all-reduce.1
where the time goes:
time: 386 us; the launch traced here: 383 us
  waiting for transfers between devices  133 us (34%)
  blocking collectives  97.5 us (25%)
  starting transfers between devices  81.3 us (21%)
  local copies, waits for them, and re-layouts  27.6 us (7%)
  other arithmetic  21.3 us (6%)
  between operations  14.6 us (4%)
  matrix products  7.98 us (2%)
    psum x1, waiting for transfers between devices, local(): lax.psum(weight_part, ('row', 'col'))  125 us
    all_to_all x1, starting transfers between devices, local(): lax.all_to_all(source_of[send_order], ('row', 'col'), split_axis=0, conca...  78.3 us
    all_to_all x1, blocking collectives, local(): lax.all_to_all(summed[send_order], ('row', 'col'), split_axis=0, concat_a...  71 us
    all_gather x1, blocking collectives, local(): group_rows = lax.all_gather(hidden, 'row', axis=0, tiled=True)  14.6 us
    unnamed x16, local copies, waits for them, and re-layouts  12.9 us
    all_gather x1, blocking collectives, local(): strip_grad = lax.all_gather(local_grad, 'col', axis=0, tiled=True)  11.8 us
    scatter-add x2, other arithmetic, add_block(): return totals.at[target].add(product)  8.72 us
  transfers between devices with their start and end apart: 5, of which 3 were waited for; matrix products, arithmetic and copies ran while one was open for 7% of the time, Pallas kernels for 0%

commit v1 on v0

--- a/solution.py
+++ b/solution.py
@@ -3,6 +3,11 @@
 import jax.numpy as jnp
 from jax import lax
 from jax.sharding import PartitionSpec as P
+
+
+def one_after_other(value, axis_one, axis_two):
+    inner = lax.psum(value, axis_one)
+    return lax.psum(inner, axis_two)
 
 
 def silu_slope(values):
@@ -103,7 +108,7 @@
         jnp.bfloat16
     )
     weight_part = jnp.dot(features.T, source_part, preferred_element_type=jnp.float32)
-    weight_grad = lax.psum(weight_part, ("row", "col")) * (
+    weight_grad = one_after_other(weight_part, "col", "row") * (
         1.0 / math.sqrt(shard_rows * group_total)
     )
     return (activations, feature_grad, weight_grad)

time: 386 us -> 352 us (0.912)
  blocking collectives: 97.5 us -> 26.5 us
  starting transfers between devices: 81.3 us -> 142 us
  waiting for transfers between devices: 133 us -> 105 us
    all_to_all x1 -> x0, blocking collectives: 71 us -> none  [local(): lax.all_to_all(summed[send_order], ('row', 'col'), split_axis=0, concat_a...]
    all_to_all x0 -> x1, starting transfers between devices: none -> 60.8 us  [local(): lax.all_to_all(summed[send_order], ('row', 'col'), split_axis=0, concat_a...]
    psum x1 -> x2, waiting for transfers between devices: 125 us -> 86.8 us  [the longest x1 53.9 us: one_after_other(): inner = lax.psum(value, axis_one)]
    reduce_scatter x1, waiting for transfers between devices: 0.88 us -> 11.6 us  [local(): lax.psum_scatter(group_partial.astype(jnp.bfloat16), 'row', scatter_dimen...]
  transfers between devices with their start and end apart: 5 -> 7, of which waited for: 3 -> 4; matrix products, arithmetic and copies ran while one was open for 7% -> 8% of each run, Pallas kernels for 0% -> 0%
where the time goes in v1:
time: 352 us; the launch traced here: 346 us
  starting transfers between devices  142 us (40%)
  waiting for transfers between devices  105 us (30%)
  local copies, waits for them, and re-layouts  28.3 us (8%)
  blocking collectives  26.5 us (8%)
  other arithmetic  21.3 us (6%)
  between operations  14.6 us (4%)
  matrix products  7.98 us (2%)
    all_to_all x1, starting transfers between devices, local(): lax.all_to_all(source_of[send_order], ('row', 'col'), split_axis=0, conca...  78.3 us
    all_to_all x1, starting transfers between devices, local(): lax.all_to_all(summed[send_order], ('row', 'col'), split_axis=0, concat_a...  60.8 us
    psum x1, waiting for transfers between devices, one_after_other(): inner = lax.psum(value, axis_one)  53.9 us
    psum x1, waiting for transfers between devices, one_after_other(): return lax.psum(inner, axis_two)  32.9 us
    all_gather x1, blocking collectives, local(): group_rows = lax.all_gather(hidden, 'row', axis=0, tiled=True)  14.6 us
    unnamed x16, local copies, waits for them, and re-layouts  12.9 us
    all_gather x1, blocking collectives, local(): strip_grad = lax.all_gather(local_grad, 'col', axis=0, tiled=True)  11.8 us
    reduce_scatter x1, waiting for transfers between devices, local(): lax.psum_scatter(group_partial.astype(jnp.bfloat16), 'row', scatter_dimen...  11.6 us
  transfers between devices with their start and end apart: 7, of which 4 were waited for; matrix products, arithmetic and copies ran while one was open for 8% of the time, Pallas kernels for 0%

profile of v1, /device:TPU:1, one launch (start us, length us, event | category | flops | bytes accessed | tf_op | source)
XLA Modules:
  0.0 346.0 jit_solution(11066530294407119655)
XLA Ops:
  8.1 0.9 convolution_convert_fusion.1
  9.0 14.6 %all_gather.6 = bf16[1536,128]{1,0:T(8,128)(2,1)} all-gather(bf16[384,128]{1,0:T(8,128)(2,1)S(1)} %convolution_convert_fusion.1), channel_id=1, replica_groups=mesh['row'=4,'col'=8] {'row'}, dimensions={0}, use_global_device_ids=true | all-gather | bytes 491520 | tf_op jit(solution)/shard_map/all_gather | solution.py:63
  23.6 1.3 broadcast_in_dim.48
  25.0 10.2 %while.20 = (s32[]{:T(128)}, f32[24,128,128]{2,1,0:T(8,128)}, s32[]{:T(128)}, s32[256]{0:T(256)S(1)}, s32[]{:T(128)}, /*index=5*/bf16[256,128,128]{2,1,0:T(8,128...) while((s32[]{:T(128)}, f32[24,128,128]{2,1,0:T(8,128)}, ...), condition=%wide.region_3.4_spmd, body=%wide.region_1.3_spmd.sunk | while | flops 135267584 | bytes 12588147 | solution.py:51
  25.7 1.7 gather_fusion
  27.5 1.7 convolution_select_fusion.4
  29.1 6.1 %scatter_fusion = f32[24,128,128]{2,1,0:T(8,128)} fusion(f32[24,128,128]{2,1,0:T(8,128)} %get-tuple-element.283, s32[32]{0:T(128)S(1)} %get-tuple-element.258, f32[32,128,128]{2,1,0:T(8,128)S(1)} %convolution_select_fusion.4), kind=kCustom, calls=%fused_computation.5.clone.1 | custom fusion | flops 524288 | bytes 6291584 | tf_op jit(solution)/shard_map/while/body/scatter-add | solution.py:48
  35.2 2.5 convert_element_type.37
  37.8 3.8 %sort.17 = (s32[384]{0:T(512)}, s32[384]{0:T(512)S(1)}) sort(s32[384]{0:T(512)S(1)} %add_select_fusion, s32[384]{0:T(512)S(1)} %iota.14), dimensions={0}, to_apply=%region_0.1 | sort | flops 3456 | bytes 6144 | tf_op jit(solution)/shard_map/jit(argsort)/sort | solution.py:78
  41.5 2.8 gather_fusion.2
  45.1 78.3 %all-to-all-start = ((s32[32,12,1]{1,2,0:T(1,128)}), s32[32,12,1]{1,2,0:T(1,128)S(1)}, u32[]{:S(2)}, u32[]{:S(2)}) async-start(s32[32,12,1]{1,2,0:T(1,128)} %bitcast), calls=%async_computation | async-start | bytes 32768 | tf_op jit(solution)/shard_map/all_to_all | solution.py:81
  123.4 6.7 %all-to-all-done = s32[32,12,1]{1,2,0:T(1,128)S(1)} async-done(((s32[32,12,1]{1,2,0:T(1,128)}), s32[32,12,1]{1,2,0:T(1,128)S(1)}, u32[]{:S(2)}, u32[]{:S(2)}) %all-to-all-start) | async-done | bytes 1568 | tf_op jit(solution)/shard_map/all_to_all | solution.py:81
  130.3 1.4 gather_fusion.4
  132.5 2.8 all-to-all-start.2
  135.3 12.0 %copy.18 = bf16[1,256,128,128]{2,3,1,0:T(8,128)(2,1)} copy(bf16[1,256,128,128]{3,2,1,0:T(8,128)(2,1)} %bitcast.28) | data formatting | bytes 16777216 | tf_op args[2]
  147.3 1.5 scatter_custom_fusion.3
  148.8 1.0 fusion.10
  149.8 11.8 %all_gather.7 = bf16[3072,128]{1,0:T(8,128)(2,1)} all-gather(bf16[384,128]{1,0:T(8,128)(2,1)S(1)} %fusion.10), channel_id=1, replica_groups=mesh['row'=4,'col'=8] {'col'}, dimensions={0}, use_global_device_ids=true | all-gather | bytes 884736 | tf_op jit(solution)/shard_map/all_gather | solution.py:94
  161.7 8.3 %while.21 = (s32[]{:T(128)}, f32[12,128,128]{2,1,0:T(8,128)S(1)}, s32[]{:T(128)}, s32[256]{0:T(256)S(1)}, s32[]{:T(128)}, /*index=5*/bf16[256,128,128]{1,2,0:T(8...) while((s32[]{:T(128)}, f32[12,128,128]{2,1,0:T(8,128)S(1)}, ...), condition=%wide.region_9.10_spmd, body=%wide.region_7.9_spmd.sunk | while | flops 135267584 | bytes 12588147 | solution.py:51
  162.5 2.9 gather_fusion.1
  165.4 2.0 convolution_select_fusion.5
  167.4 2.7 scatter_fusion.1
  170.1 0.8 convert_element_type.45
  170.9 1.4 gather_fusion.3
  173.1 60.8 %all-to-all-start.1 = ((bf16[32,12,128]{2,1,0:T(8,128)(2,1)}), bf16[32,12,128]{2,1,0:T(8,128)(2,1)S(1)}, u32[]{:S(2)}, u32[]{:S(2)}) async-start(bf16[32,12,128]{2,1,0:T(8,128)(2,1)} %all_to_all.22), calls=%async_computation.2 | async-start | bytes 262144 | tf_op jit(solution)/shard_map/all_to_all | solution.py:80
  233.9 11.6 %reduce-scatter.5.cloned.1.call-done = bf16[384,128]{1,0:T(8,128)(2,1)} async-done(((bf16[1536,128]{1,0:T(8,128)(2,1)}), bf16[384,128]{1,0:T(8,128)(2,1)}) %reduce-scatter.5.cloned.1.call-update) | async-done | bytes 98320 | tf_op jit(solution)/shard_map/reduce_scatter | solution.py:104
  245.5 1.7 convolution_bitcast_fusion
  247.3 2.1 scatter_custom_fusion.2
  249.4 53.9 %all-reduce.3.cloned.1.call-done = f32[128,128]{0,1:T(8,128)} async-done(((f32[128,128]{0,1:T(8,128)}), f32[128,128]{0,1:T(8,128)}) %all-reduce.3.cloned.1.call-update) | async-done | bytes 65552 | tf_op jit(solution)/shard_map/psum | solution.py:9
  303.3 1.7 convolution_convert_fusion
  305.0 32.9 %all-reduce.5.cloned.1.call-done = f32[128,128]{0,1:T(8,128)} async-done(((f32[128,128]{0,1:T(8,128)}), f32[128,128]{0,1:T(8,128)}) %all-reduce.5.cloned.1.call-update) | async-done | bytes 65552 | tf_op jit(solution)/shard_map/psum | solution.py:10
  337.9 0.8 broadcast_multiply_fusion
  (46 shorter events, 5.1 us)
Async XLA Ops:
  7.2 0.9 copy-start
  7.2 17.8 %copy-start.6 = (s32[1,256]{1,0:T(1,128)S(1)}, s32[1,256]{1,0:T(1,128)}, u32[]{:S(2)}) copy-start(s32[1,256]{1,0:T(1,128)} %param.16) | copy-start | bytes 3076
  7.2 17.8 %copy-start.5 = (s32[1,256]{1,0:T(1,128)S(1)}, s32[1,256]{1,0:T(1,128)}, u32[]{:S(2)}) copy-start(s32[1,256]{1,0:T(1,128)} %param.15) | copy-start | bytes 3076
  7.2 141.6 %reduce-scatter.3.cloned.1.call-start = ((), (), s32[]{:S(2)}) async-start(), calls=%async_computation.5 | async-start | bytes 884736 | tf_op jit(solution)/shard_map/reduce_scatter | solution.py:74
  35.2 2.5 copy-start.1
  37.7 92.6 %copy-start.3 = (bf16[384,128]{1,0:T(8,128)(2,1)S(1)}, bf16[384,128]{1,0:T(8,128)(2,1)}, u32[]{:S(2)}) copy-start(bf16[384,128]{1,0:T(8,128)(2,1)} %param.19) | copy-start | bytes 294916
  45.1 85.1 %all-to-all-start = ((s32[32,12,1]{1,2,0:T(1,128)}), s32[32,12,1]{1,2,0:T(1,128)S(1)}, u32[]{:S(2)}, u32[]{:S(2)}) async-start(s32[32,12,1]{1,2,0:T(1,128)} %bitcast), calls=%async_computation | async-start | bytes 32768 | tf_op jit(solution)/shard_map/all_to_all | solution.py:81
  132.5 14.8 %all-to-all-start.2 = ((bf16[32,12,128]{2,1,0:T(8,128)(2,1)}), bf16[32,12,128]{2,1,0:T(8,128)(2,1)S(1)}, u32[]{:S(2)}, u32[]{:S(2)}) async-start(bf16[32,12,128]{2,1,0:T(8,128)(2,1)} %all_to_all.24), calls=%async_computation.3 | async-start | bytes 262144 | tf_op jit(solution)/shard_map/all_to_all | solution.py:88
  135.3 110.2 %reduce-scatter.5.cloned.1.call-start = ((), (), s32[]{:S(2)}) async-start(), calls=%async_computation.6 | async-start | bytes 491520 | tf_op jit(solution)/shard_map/reduce_scatter | solution.py:104
  170.0 0.9 copy-start.2
  170.0 133.2 %copy-start.4 = (bf16[128,128]{1,0:T(8,128)(2,1)S(1)}, bf16[128,128]{1,0:T(8,128)(2,1)}, u32[]{:S(2)}) copy-start(bf16[128,128]{1,0:T(8,128)(2,1)} %param.13) | copy-start | bytes 98308
  173.1 74.2 %all-to-all-start.1 = ((bf16[32,12,128]{2,1,0:T(8,128)(2,1)}), bf16[32,12,128]{2,1,0:T(8,128)(2,1)S(1)}, u32[]{:S(2)}, u32[]{:S(2)}) async-start(bf16[32,12,128]{2,1,0:T(8,128)(2,1)} %all_to_all.22), calls=%async_computation.2 | async-start | bytes 262144 | tf_op jit(solution)/shard_map/all_to_all | solution.py:80
  233.8 69.4 %all-reduce.3.cloned.1.call-start = ((), (), s32[]{:S(2)}) async-start(), calls=%async_computation.7 | async-start | bytes 131072 | tf_op jit(solution)/shard_map/psum | solution.py:9
  247.2 90.7 %all-reduce.5.cloned.1.call-start = ((), (), s32[]{:S(2)}) async-start(), calls=%async_computation.8 | async-start | bytes 131072 | tf_op jit(solution)/shard_map/psum | solution.py:10
Sparse Core Ops, SparseCore 0:
  37.8 107.7 reduce-scatter.2
  171.0 74.3 reduce-scatter.4
  249.1 54.1 all-reduce.2
  305.4 32.4 all-reduce.4
